TPU v7x, 512 devices: a whole 4x8x8 slice. The times are simulated.
512 devices in a mesh: ctx: 64 (over z, y), tp: 8 (over x, core).
Axes of the slice: x: 4, y: 8, z: 8, core: 2. Of those that a mesh axis runs over, the one named last changes fastest.
Arguments:
- span_q: bfloat16 [8192, 8192], P('ctx', 'tp'), may hold values from -21 to 21
- span_kv: bfloat16 [2, 8192, 1024], P(None, 'ctx', 'tp'), may hold values from -20 to 20
- cache_kv: bfloat16 [2, 65536, 1024], P(None, 'ctx', 'tp'), may hold values from -20 to 20
- anchor_kv: bfloat16 [2, 2048, 1024], P(None, 'ctx', 'tp'), may hold values from -20 to 20
- block_len: int32 [64], P('ctx'), may hold values from 1 to 1024, 40960 in all
- queries: bfloat16 [128, 8192], P('ctx', 'tp'), may hold values from -21 to 21
- out_weight: bfloat16 [8192, 8192], P('tp', 'ctx'), may hold values from -0.0625 to 0.0625
Outputs:
- span_out: bfloat16 [8192, 8192], P('ctx', 'tp')
- answer: bfloat16 [128, 8192], P('tp', 'ctx')
Inputs may be any that keep to these rules, and one draw needn't show every extreme that they name: The new tokens of block c follow its block_len[c] valid cache rows.
All inputs are finite; a program needn't handle non-finite values.
Results may differ from a plain program's by a relative error of at most 0.0049.
Values may be sent and summed in bfloat16 or wider, within the bound.
A program may use at most 64 MiB of HBM per device.

v0:
```python
import math
import jax
import jax.numpy as jnp
from jax import lax
from jax.sharding import PartitionSpec as P

HD = 128
masked_score = -1e30


def all_heads(query_rows, key_rows, value_rows, visible):
    row_count = query_rows.shape[0]
    head_count = query_rows.shape[1] // HD
    score_scale = 1.0 / math.sqrt(HD)

    def per_head(head_index, running):
        maxima, totals, outputs = running
        q_head = lax.dynamic_slice_in_dim(query_rows, head_index * HD, HD, 1)
        scores = (
            jnp.einsum("qd,nd->qn", q_head, key_rows, preferred_element_type=jnp.float32)
            * score_scale
        )
        scores = jnp.where(visible, scores, masked_score)
        peak_score = jnp.max(scores, axis=1, keepdims=True)
        weights = jnp.exp(scores - peak_score)
        weight_sum = jnp.sum(weights, axis=1, keepdims=True)
        product = jnp.einsum(
            "qn,nd->qd",
            weights.astype(jnp.bfloat16),
            value_rows,
            preferred_element_type=jnp.float32,
        )
        maxima = lax.dynamic_update_slice_in_dim(maxima, peak_score, head_index, 1)
        totals = lax.dynamic_update_slice_in_dim(totals, weight_sum, head_index, 1)
        outputs = lax.dynamic_update_slice_in_dim(outputs, product, head_index * HD, 1)
        return (maxima, totals, outputs)

    initial = (
        jnp.zeros((row_count, head_count), jnp.float32),
        jnp.zeros((row_count, head_count), jnp.float32),
        jnp.zeros((row_count, head_count * HD), jnp.float32),
    )
    return lax.fori_loop(0, head_count, per_head, initial)


def local(span_q, span_kv, cache_kv, anchor_kv, block_len, queries, out_weight):
    cache_count = cache_kv.shape[1]
    span_count = span_kv.shape[1]
    length = block_len[0]
    local_kv = jnp.concatenate([cache_kv, span_kv], axis=1)
    anchor_all = lax.all_gather(anchor_kv, "ctx", axis=1, tiled=True)
    query_all = lax.all_gather(queries, "ctx", axis=0, tiled=True)
    anchor_count = anchor_all.shape[1]
    first_kv = jnp.concatenate([anchor_all, local_kv], axis=1)
    key_total = first_kv.shape[1]
    column = lax.broadcasted_iota(jnp.int32, (span_count, key_total), 1)
    query_pos = lax.broadcasted_iota(jnp.int32, (span_count, key_total), 0)
    in_cache = (column >= anchor_count) & (column < anchor_count + cache_count)
    in_span = column >= anchor_count + cache_count
    visible = jnp.where(
        in_cache,
        column - anchor_count < length,
        jnp.where(in_span, column - anchor_count - cache_count <= query_pos, True),
    )
    first_max, first_sum, first_values = all_heads(span_q, first_kv[0], first_kv[1], visible)
    span_out = (first_values / jnp.repeat(first_sum, HD, axis=1)).astype(jnp.bfloat16)
    own_count = anchor_kv.shape[1]
    second_kv = jnp.concatenate([anchor_kv, local_kv], axis=1)
    column_two = lax.broadcasted_iota(jnp.int32, (1, second_kv.shape[1]), 1)
    cache_two = (column_two >= own_count) & (column_two < own_count + cache_count)
    visible_two = jnp.where(cache_two, column_two - own_count < length, True)
    part_max, part_sum, part_values = all_heads(query_all, second_kv[0], second_kv[1], visible_two)
    global_max = lax.pmax(part_max, "ctx")
    rescale = jnp.exp(part_max - global_max)
    full_sum, full_values = lax.psum(
        (part_sum * rescale, part_values * jnp.repeat(rescale, HD, axis=1)), "ctx"
    )
    attended = (full_values / jnp.repeat(full_sum, HD, axis=1)).astype(jnp.bfloat16)
    partial_value = jnp.dot(attended, out_weight, preferred_element_type=jnp.float32)
    answer = lax.psum_scatter(partial_value, "tp", scatter_dimension=0, tiled=True).astype(
        jnp.bfloat16
    )
    return (span_out, answer)


def solution(mesh):
    placed = (
        P("ctx", "tp"),
        P(None, "ctx", "tp"),
        P(None, "ctx", "tp"),
        P(None, "ctx", "tp"),
        P("ctx"),
        P("ctx", "tp"),
        P("tp", "ctx"),
    )
    return jax.shard_map(
        local,
        mesh=mesh,
        in_specs=placed,
        out_specs=(P("ctx", "tp"), P("tp", "ctx")),
        check_vma=False,
    )
```

profile of v0, /device:TPU:16, one launch (start us, length us, event | category | flops | bytes accessed | tf_op | source)
XLA Modules:
  0.0 452.8 jit_solution(17501054155772972104)
XLA Ops:
  7.2 0.7 all-gather.3.cloned.1.call-update
  8.0 56.4 %all-gather = bf16[64,2,1024]{2,1,0:T(2,128)(2,1)S(1)} all-gather(bf16[1,2,1024]{2,1,0:T(2,128)(2,1)} %bitcast.53), channel_id=1, replica_groups=mesh['ctx'=64,'tp'=8] {'ctx'}, dimensions={0}, use_global_device_ids=true | all-gather | bytes 266240 | tf_op jit(solution)/shard_map/all_gather | solution.py:52
  65.2 0.7 constant_dynamic-update-slice_fusion.5
  66.5 27.6 %all-gather.3.cloned.1.call-done = bf16[2,2048,128]{2,1,0:T(8,128)(2,1)} async-done(((bf16[2,32,128]{2,1,0:T(8,128)(2,1)}), bf16[2,2048,128]{2,1,0:T(8,128)(2,1)}) %all-gather.3.cloned.1.call-update) | async-done | bytes 1048592 | tf_op jit(solution)/shard_map/all_gather | solution.py:51
  94.1 1.3 constant_dynamic-update-slice_fusion.2
  95.7 0.8 copy-done.1
  96.5 1.1 slice_bitcast_fusion.2
  97.6 13.0 %while.35 = (s32[]{:T(128)}, f32[128,8]{0,1:T(8,128)S(1)}, f32[128,8]{0,1:T(8,128)S(1)}, f32[128,1024]{1,0:T(8,128)S(1)}, bf16[128,1024]{1,0:T(8,128)(2,1)S(1)},...) while((s32[]{:T(128)}, f32[128,8]{0,1:T(8,128)S(1)}, ...), condition=%wide.region_7.8_spmd.clone, body=%wide.region_4.7_spmd.clone.sunk | while | flops 78662336 | bytes 2530647 | solution.py:43
  97.7 0.7 select_reduce_fusion.2
  99.3 0.7 select_reduce_fusion.2
  100.9 0.7 select_reduce_fusion.2
  102.5 0.7 select_reduce_fusion.2
  104.2 0.7 select_reduce_fusion.2
  105.8 0.7 select_reduce_fusion.2
  107.4 0.7 select_reduce_fusion.2
  109.0 0.7 select_reduce_fusion.2
  110.6 137.7 %pmax.7 = f32[128,8]{0,1:T(8,128)S(1)} all-reduce(f32[128,8]{0,1:T(8,128)S(1)} %get-tuple-element.271), channel_id=1, replica_groups=mesh['ctx'=64,'tp'=8] {'ctx'}, use_global_device_ids=true, to_apply=%region_8.9 | all-reduce | flops 1024 | bytes 8192 | tf_op jit(solution)/shard_map/pmax | solution.py:73
  248.6 0.9 bitcast_multiply_fusion
  249.8 19.4 %while.34 = (s32[]{:T(128)}, f32[128,8]{0,1:T(8,128)S(1)}, f32[128,1024]{1,0:T(8,128)S(1)}, bf16[128,1024]{1,0:T(8,128)(2,1)}, bf16[3200,128]{1,0:T(8,128)(2,1)S...) while((s32[]{:T(128)}, f32[128,8]{0,1:T(8,128)S(1)}, ...), condition=%wide.region_3.4_spmd.clone, body=%wide.region_0.3_spmd.clone.sunk | while | flops 213810944 | bytes 6681151 | solution.py:43
  249.9 1.5 fusion.46
  252.3 1.5 fusion.46
  254.7 1.5 fusion.46
  257.1 1.5 fusion.46
  259.5 1.5 fusion.46
  262.0 1.5 fusion.46
  264.4 1.5 fusion.46
  266.8 1.5 fusion.46
  269.2 138.1 %psum.15 = f32[128,8]{0,1:T(8,128)S(1)} all-reduce(f32[128,8]{0,1:T(8,128)S(1)} %get-tuple-element.354), channel_id=1, replica_groups=mesh['ctx'=64,'tp'=8] {'ctx'}, use_global_device_ids=true, to_apply=%region_10.11 | all-reduce | flops 1024 | bytes 8192 | tf_op jit(solution)/shard_map/psum | solution.py:75
  407.7 1.9 fusion.22
  409.8 0.8 fusion.21
  410.6 34.3 %reduce-scatter.2.cloned.1.call-done = f32[16,128]{1,0:T(8,128)} async-done(((f32[128,128]{1,0:T(8,128)}), f32[16,128]{1,0:T(8,128)}) %reduce-scatter.2.cloned.1.call-update) | async-done | bytes 8208 | tf_op jit(solution)/shard_map/reduce_scatter | solution.py:80
  444.9 1.3 convert_element_type.25
  (96 shorter events, 16.4 us)
Async XLA Ops:
  7.2 400.5 %copy-start = (bf16[1024,128]{1,0:T(8,128)(2,1)S(1)}, bf16[1024,128]{1,0:T(8,128)(2,1)}, u32[]{:S(2)}) copy-start(bf16[1024,128]{1,0:T(8,128)(2,1)} %param.17) | copy-start | bytes 786436
  7.2 88.2 %copy-start.2 = (bf16[2,1024,128]{2,1,0:T(8,128)(2,1)S(1)}, bf16[2,1024,128]{2,1,0:T(8,128)(2,1)}, u32[]{:S(2)}) copy-start(bf16[2,1024,128]{2,1,0:T(8,128)(2,1)} %param.13) | copy-start | bytes 1572868
  7.2 86.9 %all-gather.3.cloned.1.call-start = ((), (), s32[]{:S(2)}) async-start(), calls=%async_computation.1 | async-start | bytes 1064960 | tf_op jit(solution)/shard_map/all_gather | solution.py:51
  7.9 399.6 %all-reduce.2.cloned.1.call-start = ((), (), s32[]{:S(2)}) async-start(), calls=%async_computation.2 | async-start | bytes 1048576 | tf_op jit(solution)/shard_map/psum | solution.py:75
  66.5 29.1 %copy-start.3 = (bf16[2,128,128]{2,1,0:T(8,128)(2,1)S(1)}, bf16[2,128,128]{2,1,0:T(8,128)(2,1)}, u32[]{:S(2)}) copy-start(bf16[2,128,128]{2,1,0:T(8,128)(2,1)} %param.12) | copy-start | bytes 196612
  95.7 0.8 copy-start.1
  249.6 195.3 %reduce-scatter.2.cloned.1.call-start = ((), (), s32[]{:S(2)}) async-start(), calls=%async_computation.3 | async-start | bytes 73728 | tf_op jit(solution)/shard_map/reduce_scatter | solution.py:80
Sparse Core Ops, SparseCore 0:
  11.0 83.0 all-gather.2
  249.7 155.1 all-reduce.1
  409.7 35.1 reduce-scatter.1
where the time goes:
time: 454 us; the launch traced here: 453 us
  blocking collectives  332 us (73%)
  waiting for transfers between devices  62.6 us (14%)
  matrix products  23.1 us (5%)
  between operations  14.6 us (3%)
  other arithmetic  13.6 us (3%)
  local copies, waits for them, and re-layouts  6.12 us (1%)
    psum x1, blocking collectives, local(): lax.psum((part_sum * rescale, part_values * jnp.repeat(rescale, HD, axis=...  138 us
    pmax x1, blocking collectives, local(): global_max = lax.pmax(part_max, 'ctx')  138 us
    all_gather x1, blocking collectives, local(): query_all = lax.all_gather(queries, 'ctx', axis=0, tiled=True)  56.4 us
    reduce_scatter x1, waiting for transfers between devices, local(): lax.psum_scatter(partial_value, 'tp', scatter_dimension=0, tiled=True)  34.3 us
    all_gather x1, waiting for transfers between devices, local(): anchor_all = lax.all_gather(anchor_kv, 'ctx', axis=1, tiled=True)  27.6 us
    dot_general x16, matrix products, per_head(): jnp.einsum('qd,nd->qn', q_head, key_rows, preferred_element_type=jnp.floa...  15.1 us
  transfers between devices with their start and end apart: 3, of which 2 were waited for; matrix products, arithmetic and copies ran while one was open for 5% of the time, Pallas kernels for 0%

commit v1 on v0

--- a/solution.py
+++ b/solution.py
@@ -48,7 +48,15 @@
     span_count = span_kv.shape[1]
     length = block_len[0]
     local_kv = jnp.concatenate([cache_kv, span_kv], axis=1)
-    anchor_all = lax.all_gather(anchor_kv, "ctx", axis=1, tiled=True)
+    ways, here = (lax.axis_size("ctx"), lax.axis_index("ctx"))
+    grown, reach = (anchor_kv, 1)
+    while reach < ways:
+        theirs = lax.ppermute(grown, "ctx", [(d, d ^ reach) for d in range(ways)])
+        mine_first = jnp.concatenate([grown, theirs], axis=1)
+        theirs_first = jnp.concatenate([theirs, grown], axis=1)
+        grown = jnp.where(here & reach == 0, mine_first, theirs_first)
+        reach = 2 * reach
+    anchor_all = grown
     query_all = lax.all_gather(queries, "ctx", axis=0, tiled=True)
     anchor_count = anchor_all.shape[1]
     first_kv = jnp.concatenate([anchor_all, local_kv], axis=1)

time: 454 us -> 463 us (1.020)
  the two profiles are of different devices: /device:TPU:16 before, /device:TPU:8 now
where the time goes in v1:
time: 463 us; the launch traced here: 462 us
  blocking collectives  331 us (71%)
  waiting for transfers between devices  53.2 us (11%)
  matrix products  22.9 us (5%)
  starting transfers between devices  20.5 us (4%)
  between operations  15 us (3%)
  other arithmetic  13.7 us (3%)
  local copies, waits for them, and re-layouts  4.7 us (1%)
    psum x1, blocking collectives, local(): lax.psum((part_sum * rescale, part_values * jnp.repeat(rescale, HD, axis=...  140 us
    pmax x1, blocking collectives, local(): global_max = lax.pmax(part_max, 'ctx')  139 us
    all_gather x1, blocking collectives, local(): query_all = lax.all_gather(queries, 'ctx', axis=0, tiled=True)  51.6 us
    reduce_scatter x1, waiting for transfers between devices, local(): lax.psum_scatter(partial_value, 'tp', scatter_dimension=0, tiled=True)  31.9 us
    ppermute x6, waiting for transfers between devices, local(): theirs = lax.ppermute(grown, 'ctx', [(d, d ^ reach) for d in range(ways)])  21.3 us
    ppermute x6, starting transfers between devices, local(): theirs = lax.ppermute(grown, 'ctx', [(d, d ^ reach) for d in range(ways)])  20.4 us
    dot_general x16, matrix products, per_head(): jnp.einsum('qd,nd->qn', q_head, key_rows, preferred_element_type=jnp.floa...  15 us
  transfers between devices with their start and end apart: 8, of which 4 were waited for; matrix products, arithmetic and copies ran while one was open for 4% of the time, Pallas kernels for 0%

profile of v1, /device:TPU:8, one launch (start us, length us, event | category | flops | bytes accessed | tf_op | source)
XLA Modules:
  0.0 461.9 jit_solution(14460880291155599596)
XLA Ops:
  7.2 7.8 %collective-permute-start = (bf16[2,32,128]{2,1,0:T(8,128)(2,1)}, bf16[2,32,128]{2,1,0:T(8,128)(2,1)S(1)}, u32[]{:S(2)}, u32[]{:S(2)}) collective-permute-start(bf16[2,32,128]{2,1,0:T(8,128)(2,1)} %param.14), channel_id=1, source_target_pairs={{0,8},{8,0},{16,24},{24,16},{32,40},{40,32},{48,56},{56,48},{64,72... | collective-permute-start | bytes 49160 | tf_op jit(solution)/shard_map/ppermute | solution.py:54
  15.1 0.7 constant_dynamic-update-slice_fusion.2
  15.8 1.1 constant_dynamic-update-slice_fusion.1
  16.9 0.9 constant_dynamic-update-slice_fusion
  17.8 51.6 %all-gather = bf16[64,2,1024]{2,1,0:T(2,128)(2,1)S(1)} all-gather(bf16[1,2,1024]{2,1,0:T(2,128)(2,1)S(1)} %bitcast.53), channel_id=1, replica_groups=mesh['ctx'=64,'tp'=8] {'ctx'}, dimensions={0}, use_global_device_ids=true | all-gather | bytes 266240 | tf_op jit(solution)/shard_map/all_gather | solution.py:60
  69.6 4.0 collective-permute-start.1
  73.6 13.0 %while.35 = (s32[]{:T(128)}, f32[128,8]{0,1:T(8,128)S(1)}, f32[128,8]{0,1:T(8,128)S(1)}, f32[128,1024]{1,0:T(8,128)S(1)}, bf16[128,1024]{1,0:T(8,128)(2,1)S(1)},...) while((s32[]{:T(128)}, f32[128,8]{0,1:T(8,128)S(1)}, ...), condition=%wide.region_7.8_spmd.clone, body=%wide.region_4.7_spmd.clone.sunk | while | flops 78662336 | bytes 2530647 | solution.py:43
  80.1 0.7 select_reduce_fusion.2
  81.8 0.7 select_reduce_fusion.2
  86.6 139.2 %pmax.7 = f32[128,8]{0,1:T(8,128)S(1)} all-reduce(f32[128,8]{0,1:T(8,128)S(1)} %get-tuple-element.271), channel_id=1, replica_groups=mesh['ctx'=64,'tp'=8] {'ctx'}, use_global_device_ids=true, to_apply=%region_8.9 | all-reduce | flops 1024 | bytes 8192 | tf_op jit(solution)/shard_map/pmax | solution.py:81
  225.9 1.9 collective-permute-start.2
  227.9 8.1 %collective-permute-done.2 = bf16[2,128,128]{2,1,0:T(8,128)(2,1)S(1)} collective-permute-done((bf16[2,128,128]{2,1,0:T(8,128)(2,1)S(1)}, bf16[2,128,128]{2,1,0:T(8,128)(2,1)S(1)}, u32[]{:S(2)}, u32[]{:S(2)}) %collective-permute-start.2) | collective-permute-done | bytes 65568 | tf_op jit(solution)/shard_map/ppermute | solution.py:54
  236.0 1.9 collective-permute-start.3
  238.2 0.9 bitcast_multiply_fusion
  239.2 3.7 collective-permute-done.3
  243.0 1.9 collective-permute-start.4
  245.6 9.5 %collective-permute-done.4 = bf16[2,512,128]{2,1,0:T(8,128)(2,1)S(1)} collective-permute-done((bf16[2,512,128]{2,1,0:T(8,128)(2,1)S(1)}, bf16[2,512,128]{2,1,0:T(8,128)(2,1)S(1)}, u32[]{:S(2)}, u32[]{:S(2)}) %collective-permute-start.4) | collective-permute-done | bytes 262176 | tf_op jit(solution)/shard_map/ppermute | solution.py:54
  255.3 2.9 collective-permute-start.5
  258.2 140.4 %psum.15 = f32[128,8]{0,1:T(8,128)S(1)} all-reduce(f32[128,8]{0,1:T(8,128)S(1)} %get-tuple-element.354), channel_id=1, replica_groups=mesh['ctx'=64,'tp'=8] {'ctx'}, use_global_device_ids=true, to_apply=%region_10.11 | all-reduce | flops 1024 | bytes 8192 | tf_op jit(solution)/shard_map/psum | solution.py:83
  399.0 1.9 fusion.22
  400.9 31.9 %reduce-scatter.2.cloned.1.call-done = f32[16,128]{1,0:T(8,128)} async-done(((f32[128,128]{1,0:T(8,128)}), f32[16,128]{1,0:T(8,128)}) %reduce-scatter.2.cloned.1.call-update) | async-done | bytes 8208 | tf_op jit(solution)/shard_map/reduce_scatter | solution.py:88
  432.8 1.3 convert_element_type.25
  434.7 19.2 %while.34 = (s32[]{:T(128)}, f32[128,8]{0,1:T(8,128)S(1)}, f32[128,1024]{1,0:T(8,128)S(1)}, bf16[128,1024]{1,0:T(8,128)(2,1)}, bf16[3200,128]{1,0:T(8,128)(2,1)S...) while((s32[]{:T(128)}, f32[128,8]{0,1:T(8,128)S(1)}, ...), condition=%wide.region_3.4_spmd.clone, body=%wide.region_0.3_spmd.clone.sunk | while | flops 213810944 | bytes 6677567 | solution.py:43
  434.7 1.5 fusion.46
  437.1 1.5 fusion.46
  439.5 1.5 fusion.46
  441.9 1.5 fusion.46
  444.3 1.5 fusion.46
  446.7 1.5 fusion.46
  449.1 1.5 fusion.46
  451.5 1.5 fusion.46
  454.2 0.8 fusion.21
  (113 shorter events, 20.3 us)
Async XLA Ops:
  7.2 391.8 %copy-start = (bf16[1024,128]{1,0:T(8,128)(2,1)S(1)}, bf16[1024,128]{1,0:T(8,128)(2,1)}, u32[]{:S(2)}) copy-start(bf16[1024,128]{1,0:T(8,128)(2,1)} %param.17) | copy-start | bytes 786436
  7.2 62.4 %copy-start.3 = (bf16[2,32,128]{2,1,0:T(8,128)(2,1)S(1)}, bf16[2,32,128]{2,1,0:T(8,128)(2,1)}, u32[]{:S(2)}) copy-start(bf16[2,32,128]{2,1,0:T(8,128)(2,1)} %param.14) | copy-start | bytes 49156
  7.2 10.6 %copy-start.4 = (bf16[2,1024]{1,0:T(2,128)(2,1)S(1)}, bf16[2,1024]{1,0:T(2,128)(2,1)}, u32[]{:S(2)}) copy-start(bf16[2,1024]{1,0:T(2,128)(2,1)} %param.16) | copy-start | bytes 12292
  7.2 391.5 %all-reduce.2.cloned.1.call-start = ((), (), s32[]{:S(2)}) async-start(), calls=%async_computation.1 | async-start | bytes 1048576 | tf_op jit(solution)/shard_map/psum | solution.py:83
  7.2 62.3 %collective-permute-start = (bf16[2,32,128]{2,1,0:T(8,128)(2,1)}, bf16[2,32,128]{2,1,0:T(8,128)(2,1)S(1)}, u32[]{:S(2)}, u32[]{:S(2)}) collective-permute-start(bf16[2,32,128]{2,1,0:T(8,128)(2,1)} %param.14), channel_id=1, source_target_pairs={{0,8},{8,0},{16,24},{24,16},{32,40},{40,32},{48,56},{56,48},{64,72... | collective-permute-start | bytes 49160 | tf_op jit(solution)/shard_map/ppermute | solution.py:54
  69.6 156.3 %collective-permute-start.1 = (bf16[2,64,128]{2,1,0:T(8,128)(2,1)S(1)}, bf16[2,64,128]{2,1,0:T(8,128)(2,1)S(1)}, u32[]{:S(2)}, u32[]{:S(2)}) collective-permute-start(bf16[2,64,128]{2,1,0:T(8,128)(2,1)S(1)} %maximum_select_fusion.5), channel_id=1, source_target_pairs={{0,16},{8,24},{16,0},{24,8},{32,48},{40,56},{48,32},{56,40},{64,80... | collective-permute-start | bytes 98312 | tf_op jit(solution)/shard_map/ppermute | solution.py:54
  225.9 10.1 %collective-permute-start.2 = (bf16[2,128,128]{2,1,0:T(8,128)(2,1)S(1)}, bf16[2,128,128]{2,1,0:T(8,128)(2,1)S(1)}, u32[]{:S(2)}, u32[]{:S(2)}) collective-permute-start(bf16[2,128,128]{2,1,0:T(8,128)(2,1)S(1)} %maximum_select_fusion.4), channel_id=1, source_target_pairs={{0,32},{8,40},{16,48},{24,56},{32,0},{40,8},{48,16},{56,24},{64,96... | collective-permute-start | bytes 196616 | tf_op jit(solution)/shard_map/ppermute | solution.py:54
  236.0 6.9 %collective-permute-start.3 = (bf16[2,256,128]{2,1,0:T(8,128)(2,1)S(1)}, bf16[2,256,128]{2,1,0:T(8,128)(2,1)S(1)}, u32[]{:S(2)}, u32[]{:S(2)}) collective-permute-start(bf16[2,256,128]{2,1,0:T(8,128)(2,1)S(1)} %maximum_select_fusion.3), channel_id=1, source_target_pairs={{0,64},{8,72},{16,80},{24,88},{32,96},{40,104},{48,112},{56,120},{... | collective-permute-start | bytes 393224 | tf_op jit(solution)/shard_map/ppermute | solution.py:54
  239.1 193.6 %reduce-scatter.2.cloned.1.call-start = ((), (), s32[]{:S(2)}) async-start(), calls=%async_computation.2 | async-start | bytes 73728 | tf_op jit(solution)/shard_map/reduce_scatter | solution.py:88
  243.0 12.1 %collective-permute-start.4 = (bf16[2,512,128]{2,1,0:T(8,128)(2,1)S(1)}, bf16[2,512,128]{2,1,0:T(8,128)(2,1)S(1)}, u32[]{:S(2)}, u32[]{:S(2)}) collective-permute-start(bf16[2,512,128]{2,1,0:T(8,128)(2,1)S(1)} %maximum_select_fusion.2), channel_id=1, source_target_pairs={{0,128},{8,136},{16,144},{24,152},{32,160},{40,168},{48,176},{56,1... | collective-permute-start | bytes 786440 | tf_op jit(solution)/shard_map/ppermute | solution.py:54
  255.3 178.8 %collective-permute-start.5 = (bf16[2,1024,128]{2,1,0:T(8,128)(2,1)S(1)}, bf16[2,1024,128]{2,1,0:T(8,128)(2,1)S(1)}, u32[]{:S(2)}, u32[]{:S(2)}) collective-permute-start(bf16[2,1024,128]{2,1,0:T(8,128)(2,1)S(1)} %maximum_select_fusion.1), channel_id=1, source_target_pairs={{0,256},{8,264},{16,272},{24,280},{32,288},{40,296},{48,304},{56,3... | collective-permute-start | bytes 1572872 | tf_op jit(solution)/shard_map/ppermute | solution.py:54
  400.9 33.5 %copy-start.1 = (bf16[2,1024,128]{2,1,0:T(8,128)(2,1)S(1)}, bf16[2,1024,128]{2,1,0:T(8,128)(2,1)}, u32[]{:S(2)}) copy-start(bf16[2,1024,128]{2,1,0:T(8,128)(2,1)} %param.13) | copy-start | bytes 1572868
  400.9 33.5 %copy-start.2 = (bf16[2,128,128]{2,1,0:T(8,128)(2,1)S(1)}, bf16[2,128,128]{2,1,0:T(8,128)(2,1)}, u32[]{:S(2)}) copy-start(bf16[2,128,128]{2,1,0:T(8,128)(2,1)} %param.12) | copy-start | bytes 196612
Sparse Core Ops, SparseCore 0:
  239.3 156.0 all-reduce.1
  401.0 31.7 reduce-scatter.1
